TPU v7x, 32 devices: a whole 2x2x4 slice. The times are simulated.
32 devices in a mesh: region: 16 (over z, y, core), freq: 2 (over x).
Axes of the slice: x: 2, y: 2, z: 4, core: 2. Of those that a mesh axis runs over, the one named last changes fastest.
Arguments:
- dirty_map: float32 [4, 16384], P('freq', 'region'), may hold values from -6 to 6
- psf_blocks: bfloat16 [4, 128, 7, 128, 128], P('freq', 'region'), as said below
- col_index: int32 [128, 7], P('region'), may hold values from 0 to 127, as said below
- block_live: int32 [128, 7], P('region'), may hold values from 0 to 1, as said below
Outputs:
- source_map: float32 [4, 16384], P('freq', 'region')
- broadband: float32 [16384], P('region')
Inputs may be any that keep to these rules, and one draw needn't show every extreme that they name: `col_index`: block row i stores itself in slot 0; the pattern is symmetric: if row i names j then row j names i, and column offsets are the same for every row (mod 128). `block_live`: slot 0 is always 1; the flag of block (i, j) equals that of block (j, i). `psf_blocks`: the operator is symmetric: the block of row i naming column j is the transpose of the block of row j naming column i; diagonal entries of slot 0 lie between 0.9 and 1.1.
All inputs are finite; a program needn't handle non-finite values.
Results may differ from a plain program's by a relative error of at most 0.0032.
Values may be sent and summed in bfloat16 or wider, within the bound.
A program may use at most 64 MiB of HBM per device.

v0:
```python
import jax
import jax.numpy as jnp
from jax import lax
from jax.sharding import PartitionSpec as P

ITERS = 3


def local(dirty_map, psf_blocks, col_index, block_live):
    freq_count = psf_blocks.shape[0]
    row_blocks = psf_blocks.shape[1]
    block_width = psf_blocks.shape[3]
    diagonal = jnp.diagonal(psf_blocks[:, :, 0], axis1=2, axis2=3).astype(jnp.float32)
    target = dirty_map.reshape(freq_count, row_blocks, block_width)
    alive_mask = block_live.astype(jnp.bfloat16)
    estimate = jnp.maximum(0.0, target / diagonal)
    for iteration in range(ITERS):
        coarse = estimate.astype(jnp.bfloat16)
        gathered = lax.all_gather(coarse, "region", axis=1, tiled=True)
        picked = gathered[:, col_index, :] * alive_mask[None, :, :, None]
        applied = jnp.einsum(
            "fbkpq,fbkq->fbp", psf_blocks, picked, preferred_element_type=jnp.float32
        )
        estimate = jnp.maximum(0.0, estimate + (target - applied) / diagonal)
    broadband = lax.psum(jnp.sum(estimate, axis=0).reshape(-1), "freq")
    return (estimate.reshape(freq_count, row_blocks * block_width), broadband)


def solution(mesh):
    return jax.shard_map(
        local,
        mesh=mesh,
        in_specs=(
            P("freq", "region"),
            P("freq", "region", None, None, None),
            P("region", None),
            P("region", None),
        ),
        out_specs=(P("freq", "region"), P("region")),
        check_vma=False,
    )
```

profile of v0, /device:TPU:0, one launch (start us, length us, event | category | flops | bytes accessed | tf_op | source)
XLA Modules:
  0.0 93.3 jit_solution(370257853647034112)
XLA Ops:
  0.6 1.1 %slice.3 = bf16[2,8,1,128,128]{4,3,2,1,0:T(8,128)(2,1)S(1)} slice(bf16[2,8,7,128,128]{4,3,2,1,0:T(8,128)(2,1)} %param.5), slice={[0:2], [0:8], [0:1], [0:128], [0:128]} | slice | bytes 1048576 | tf_op jit(solution)/shard_map/slice | solution.py:13
  1.7 0.0 copy-start
  1.7 0.0 copy-start.2
  1.7 0.0 copy-start.1
  1.8 9.1 %copy.52 = bf16[2,8,1,128,128]{1,0,4,3,2:T(2,128)(2,1)} copy(bf16[2,8,1,128,128]{4,3,2,1,0:T(8,128)(2,1)S(1)} %slice.3) | data formatting | bytes 1048576
  10.8 4.3 %gather_fusion = bf16[128,2,8]{2,1,0:T(2,128)(2,1)S(1)} fusion(bf16[2,8,128,128]{1,0,3,2:T(2,128)(2,1)} %bitcast.96, s32[128]{0:T(128)S(1)} %or_bitcast_fusion), kind=kCustom, calls=%fused_computation | custom fusion | bytes 9216 | tf_op jit(solution)/shard_map/jit(diagonal)/gather | solution.py:13
  15.1 0.1 copy.39
  15.2 0.0 copy-done
  15.2 23.3 %all_gather.9 = bf16[2,128,128]{2,0,1:T(2,128)(2,1)S(1)} all-gather(bf16[2,8,128]{2,0,1:T(2,128)(2,1)S(1)} %copy.40), channel_id=1, replica_groups=mesh['region'=16,'freq'=2] {'region'}, dimensions={1}, use_global_device_ids=true | all-gather | bytes 69632 | tf_op jit(solution)/shard_map/all_gather | solution.py:19
  38.5 0.0 copy-done.2
  38.5 0.1 reshape.25
  38.6 0.6 gather_fusion.1
  39.2 0.0 copy-done.1
  39.2 0.1 multiply_bitcast_fusion.2
  39.4 3.2 %fusion.4 = f32[2,8,1,128,1]{3,2,4,1,0:T(1,128)S(1)} fusion(bf16[2,8,7,128,128]{4,3,2,1,0:T(8,128)(2,1)} %param.5, bf16[2,8,7,128,1]{3,0,2,1,4:T(2,128)(2,1)S(1)} %multiply_bitcast_fusion.2), kind=kOutput, calls=%fused_computation.8 | convolution fusion | flops 3670016 | bytes 3706880 | tf_op jit(solution)/shard_map/fbkpq,fbkq->fbp/dot_general | solution.py:21
  42.6 17.6 %all_gather.10 = bf16[2,128,128]{2,0,1:T(2,128)(2,1)S(1)} all-gather(bf16[2,8,128]{2,0,1:T(2,128)(2,1)S(1)} %copy.41), channel_id=1, replica_groups=mesh['region'=16,'freq'=2] {'region'}, dimensions={1}, use_global_device_ids=true | all-gather | bytes 69632 | tf_op jit(solution)/shard_map/all_gather | solution.py:19
  60.2 0.6 gather_fusion.2
  60.9 0.1 multiply_bitcast_fusion.1
  61.0 3.2 %fusion.2 = f32[2,8,1,128,1]{3,2,4,1,0:T(1,128)S(1)} fusion(bf16[2,8,7,128,128]{4,3,2,1,0:T(8,128)(2,1)} %param.5, bf16[2,8,7,128,1]{3,0,2,1,4:T(2,128)(2,1)S(1)} %multiply_bitcast_fusion.1), kind=kOutput, calls=%fused_computation.6 | convolution fusion | flops 3670016 | bytes 3706880 | tf_op jit(solution)/shard_map/fbkpq,fbkq->fbp/dot_general | solution.py:21
  64.3 18.9 %all_gather.11 = bf16[2,128,128]{2,0,1:T(2,128)(2,1)S(1)} all-gather(bf16[2,8,128]{2,0,1:T(2,128)(2,1)S(1)} %copy.42), channel_id=1, replica_groups=mesh['region'=16,'freq'=2] {'region'}, dimensions={1}, use_global_device_ids=true | all-gather | bytes 69632 | tf_op jit(solution)/shard_map/all_gather | solution.py:19
  83.2 0.6 gather_fusion.3
  83.8 0.1 multiply_bitcast_fusion
  84.0 3.2 %fusion = f32[2,8,1,128,1]{3,2,4,1,0:T(1,128)S(1)} fusion(bf16[2,8,7,128,128]{4,3,2,1,0:T(8,128)(2,1)} %param.5, bf16[2,8,7,128,1]{3,0,2,1,4:T(2,128)(2,1)S(1)} %multiply_bitcast_fusion), kind=kOutput, calls=%fused_computation.4 | convolution fusion | flops 3670016 | bytes 3706880 | tf_op jit(solution)/shard_map/fbkpq,fbkq->fbp/dot_general | solution.py:21
  87.2 0.6 copy.77
  87.8 5.5 %psum.7 = f32[1024]{0:T(1024)} all-reduce(f32[1024]{0:T(1024)S(1)} %bitcast.111), channel_id=1, replica_groups=mesh['region'=16,'freq'=2] {'freq'}, use_global_device_ids=true, to_apply=%region_1.2 | all-reduce | flops 1024 | bytes 8192 | tf_op jit(solution)/shard_map/psum | solution.py:25
  (11 shorter events, 0.2 us)
Async XLA Ops:
  1.7 13.4 %copy-start = (f32[2,1024]{1,0:T(2,128)S(1)}, f32[2,1024]{1,0:T(2,128)}, u32[]{:S(2)}) copy-start(f32[2,1024]{1,0:T(2,128)} %param.4) | copy-start | bytes 24580
  1.7 36.7 %copy-start.2 = (s32[8,7]{1,0:T(8,128)S(1)}, s32[8,7]{1,0:T(8,128)}, u32[]{:S(2)}) copy-start(s32[8,7]{1,0:T(8,128)} %param.6) | copy-start | bytes 676
  1.7 37.5 %copy-start.1 = (s32[8,7]{1,0:T(8,128)S(1)}, s32[8,7]{1,0:T(8,128)}, u32[]{:S(2)}) copy-start(s32[8,7]{1,0:T(8,128)} %param.7) | copy-start | bytes 676
where the time goes:
time: 93.7 us; the launch traced here: 93.3 us
  blocking collectives  65.3 us (70%)
  local copies, waits for them, and re-layouts  17.1 us (18%)
  matrix products  9.66 us (10%)
    all_gather x3, blocking collectives, local(): gathered = lax.all_gather(coarse, 'region', axis=1, tiled=True)  59.8 us
    unnamed x8, local copies, waits for them, and re-layouts  9.69 us
    dot_general x3, matrix products, local(): jnp.einsum('fbkpq,fbkq->fbp', psf_blocks, picked, preferred_element_type=...  9.66 us
    psum x1, blocking collectives, local(): broadband = lax.psum(jnp.sum(estimate, axis=0).reshape(-1), 'freq')  5.5 us
    gather x2, local copies, waits for them, and re-layouts, local(): jnp.diagonal(psf_blocks[:, :, 0], axis1=2, axis2=3).astype(jnp.float32)  4.32 us
    gather x3, local copies, waits for them, and re-layouts, local(): picked = gathered[:, col_index, :] * alive_mask[None, :, :, None]  1.9 us

commit v1 on v0

v1 whole, which is shorter than its diff:
```python
import functools

import jax
import jax.numpy as jnp
from jax import lax
from jax.experimental import pallas as pl
from jax.experimental.pallas import tpu as pltpu
from jax.sharding import PartitionSpec as P

ITERS = 3
MESH = pl.DeviceIdType.MESH
TRANSPOSED = (((1,), (1,)), ((), ()))


def kernel(
    regions,
    groups,
    dirty_ref,
    psf_hbm,
    col_ref,
    live_ref,
    est_ref,
    broad_ref,
    psf,
    target_ref,
    outgoing,
    arrived,
    spread,
    picked,
    partial,
    load_sem,
    send_sem,
    recv_sem,
    broad_send,
    broad_recv,
):
    me = lax.axis_index("region")
    group = lax.axis_index("freq")
    freq_count, row_blocks, slots, width = psf.shape[:4]
    rows = freq_count * row_blocks

    first = pltpu.make_async_copy(
        psf_hbm.at[:, :, pl.ds(0, 1)], psf.at[:, :, pl.ds(0, 1)], load_sem.at[0]
    )
    rest = pltpu.make_async_copy(
        psf_hbm.at[:, :, pl.ds(1, slots - 1)], psf.at[:, :, pl.ds(1, slots - 1)], load_sem.at[1]
    )
    first.start()
    rest.start()
    barrier = pltpu.get_barrier_semaphore()
    for step in range(1, regions):
        pl.semaphore_signal(
            barrier, inc=1, device_id={"region": lax.rem(me + step, regions)}, device_id_type=MESH
        )
    for step in range(1, groups):
        pl.semaphore_signal(
            barrier, inc=1, device_id={"freq": lax.rem(group + step, groups)}, device_id_type=MESH
        )

    for f in range(freq_count):
        for i in range(row_blocks):
            row = f * row_blocks + i
            target_ref[row : row + 1, :] = dirty_ref[f : f + 1, i * width : (i + 1) * width]
    target = target_ref[...]
    alive = [
        jnp.concatenate(
            [jnp.broadcast_to(live_ref[:, k : k + 1].astype(jnp.float32), (row_blocks, width))] * freq_count,
            axis=0,
        )
        for k in range(1, slots)
    ]
    alive = jnp.concatenate(alive, axis=1)
    row_ids = lax.broadcasted_iota(jnp.int32, (rows, width), 0)

    first.wait()
    eye = lax.broadcasted_iota(jnp.int32, (width, width), 0) == lax.broadcasted_iota(
        jnp.int32, (width, width), 1
    )
    diagonal = jnp.zeros((rows, width), jnp.float32)
    for f in range(freq_count):
        for i in range(row_blocks):
            block = psf[f, i, 0].astype(jnp.float32)
            line = jnp.sum(jnp.where(eye, block, 0.0), axis=0, keepdims=True)
            diagonal = jnp.where(row_ids == f * row_blocks + i, line, diagonal)
    estimate = jnp.maximum(0.0, target / diagonal)

    for iteration in range(ITERS):
        coarse = estimate.astype(jnp.bfloat16)
        outgoing[iteration] = coarse
        if iteration == 0:
            pl.semaphore_wait(barrier, regions - 1 + groups - 1)
        for step in range(1, regions):
            pltpu.make_async_remote_copy(
                src_ref=outgoing.at[iteration],
                dst_ref=arrived.at[iteration, me],
                send_sem=send_sem.at[iteration],
                recv_sem=recv_sem.at[iteration],
                device_id={"region": lax.rem(me + step, regions)},
                device_id_type=MESH,
            ).start()
        applied = jnp.zeros((rows, width), jnp.float32)
        for f in range(freq_count):
            for i in range(row_blocks):
                product = lax.dot_general(
                    coarse, psf[f, i, 0], TRANSPOSED, preferred_element_type=jnp.float32
                )
                applied = jnp.where(row_ids == f * row_blocks + i, product, applied)
        if iteration == 0:
            rest.wait()
        others = arrived.at[iteration, pl.ds(0, regions - 1)]
        pltpu.make_async_copy(others, others, recv_sem.at[iteration]).wait()
        arrived[iteration, me] = coarse
        spread[...] = arrived[iteration].astype(jnp.float32)
        for i in range(row_blocks):
            for k in range(1, slots):
                column = col_ref[i, k]
                owner = column // row_blocks
                inner = column % row_blocks
                for f in range(freq_count):
                    row = f * row_blocks + i
                    picked[row : row + 1, (k - 1) * width : k * width] = spread[
                        owner, pl.ds(f * row_blocks + inner, 1), :
                    ]
        chosen = (picked[...] * alive).astype(jnp.bfloat16)
        far = jnp.zeros((rows, width), jnp.float32)
        for f in range(freq_count):
            for i in range(row_blocks):
                blocks = jnp.concatenate([psf[f, i, k] for k in range(1, slots)], axis=1)
                product = lax.dot_general(
                    chosen, blocks, TRANSPOSED, preferred_element_type=jnp.float32
                )
                far = jnp.where(row_ids == f * row_blocks + i, product, far)
        estimate = jnp.maximum(0.0, estimate + (target - (applied + far)) / diagonal)

    local_sum = estimate[:row_blocks]
    for f in range(1, freq_count):
        local_sum = local_sum + estimate[f * row_blocks : (f + 1) * row_blocks]
    partial[group] = local_sum
    broad = []
    for step in range(1, groups):
        copy = pltpu.make_async_remote_copy(
            src_ref=partial.at[group],
            dst_ref=partial.at[group],
            send_sem=broad_send.at[step],
            recv_sem=broad_recv.at[step],
            device_id={"freq": lax.rem(group + step, groups)},
            device_id_type=MESH,
        )
        copy.start()
        broad.append(copy)
    est_ref[...] = estimate
    for iteration in range(ITERS):
        others = arrived.at[iteration, pl.ds(0, regions - 1)]
        pltpu.make_async_copy(others, others, send_sem.at[iteration]).wait()
    for copy in broad:
        copy.wait()
    total = partial[0]
    for g in range(1, groups):
        total = total + partial[g]
    broad_ref[...] = total


def solution(mesh):
    regions, groups = mesh.shape["region"], mesh.shape["freq"]

    def local(dirty_map, psf_blocks, col_index, block_live):
        freq_count, row_blocks, slots, width, _ = psf_blocks.shape
        rows = freq_count * row_blocks
        vmem = pl.BlockSpec(memory_space=pltpu.VMEM)
        estimate, broadband = pl.pallas_call(
            functools.partial(kernel, regions, groups),
            out_shape=(
                jax.ShapeDtypeStruct((rows, width), jnp.float32),
                jax.ShapeDtypeStruct((row_blocks, width), jnp.float32),
            ),
            in_specs=[
                vmem,
                pl.BlockSpec(memory_space=pl.ANY),
                pl.BlockSpec(memory_space=pltpu.SMEM),
                vmem,
            ],
            out_specs=(vmem, vmem),
            scratch_shapes=[
                pltpu.VMEM(psf_blocks.shape, jnp.bfloat16),
                pltpu.VMEM((rows, width), jnp.float32),
                pltpu.VMEM((ITERS, rows, width), jnp.bfloat16),
                pltpu.VMEM((ITERS, regions, rows, width), jnp.bfloat16),
                pltpu.VMEM((regions, rows, width), jnp.float32),
                pltpu.VMEM((rows, (slots - 1) * width), jnp.float32),
                pltpu.VMEM((groups, row_blocks, width), jnp.float32),
                pltpu.SemaphoreType.DMA((2,)),
                pltpu.SemaphoreType.DMA((ITERS,)),
                pltpu.SemaphoreType.DMA((ITERS,)),
                pltpu.SemaphoreType.DMA((groups,)),
                pltpu.SemaphoreType.DMA((groups,)),
            ],
            compiler_params=pltpu.CompilerParams(collective_id=0, has_side_effects=True),
        )(dirty_map, psf_blocks, col_index, block_live)
        return estimate.reshape(freq_count, row_blocks * width), broadband.reshape(-1)

    return jax.shard_map(
        local,
        mesh=mesh,
        in_specs=(
            P("freq", "region"),
            P("freq", "region", None, None, None),
            P("region", None),
            P("region", None),
        ),
        out_specs=(P("freq", "region"), P("region")),
        check_vma=False,
    )
```

time: 93.7 us -> 28.7 us (0.31)
  blocking collectives: 65.3 us -> 0 us
  Pallas kernels: 0 us -> 25.2 us
  local copies, waits for them, and re-layouts: 17.1 us -> 2.57 us
  matrix products: 9.66 us -> 0 us
    all_gather x3 -> x0, blocking collectives: 59.8 us -> none  [local(): gathered = lax.all_gather(coarse, 'region', axis=1, tiled=True)]
    pallas_call x0 -> x1, Pallas kernels: none -> 25.2 us  [local(): pl.pallas_call(functools.partial(kernel, regions, groups), out_shape=(jax...]
    dot_general x3 -> x0, matrix products: 9.66 us -> none  [local(): jnp.einsum('fbkpq,fbkq->fbp', psf_blocks, picked, preferred_element_type=...]
    unnamed x8 -> x1, local copies, waits for them, and re-layouts: 9.69 us -> 1.26 us
    gather x5 -> x0, local copies, waits for them, and re-layouts: 6.22 us -> none  [the longest x2 4.32 us: local(): jnp.diagonal(psf_blocks[:, :, 0], axis1=2, axis2=3).astype(jnp.float32)]
    psum x1 -> x0, blocking collectives: 5.5 us -> none  [local(): broadband = lax.psum(jnp.sum(estimate, axis=0).reshape(-1), 'freq')]
    reshape x0 -> x1, local copies, waits for them, and re-layouts: none -> 1.3 us  [local(): estimate.reshape(freq_count, row_blocks * width)]
    slice x1 -> x0, local copies, waits for them, and re-layouts: 1.08 us -> none  [local(): psf_blocks[:, :, 0]]
where the time goes in v1:
time: 28.7 us; the launch traced here: 28.4 us
  Pallas kernels  25.2 us (88%)
  local copies, waits for them, and re-layouts  2.57 us (9%)
  between operations  0.64 us (2%)
    pallas_call x1, Pallas kernels, local(): pl.pallas_call(functools.partial(kernel, regions, groups), out_shape=(jax...  25.2 us
    reshape x1, local copies, waits for them, and re-layouts, local(): estimate.reshape(freq_count, row_blocks * width)  1.3 us
    unnamed x1, local copies, waits for them, and re-layouts  1.26 us

profile of v1, /device:TPU:0, one launch (start us, length us, event | category | flops | bytes accessed | tf_op | source)
XLA Modules:
  0.0 28.4 jit_solution(4125155541353709420)
XLA Ops:
  0.6 25.2 %shard_map.59 = (f32[16,128]{1,0:T(8,128)}, f32[8,128]{1,0:T(8,128)}) custom-call(f32[2,1024]{1,0:T(2,128)} %dirty_ref.1, bf16[2,8,7,128,128]{4,3,2,1,0:T(8,128)(2,1)} %psf_hbm.1, s32[8,7]{1,0:T(8,128)} %col_ref.1, s32[8,7]{1,0:T(8,128)} %live_ref.1), custom_call_target="tpu_custom_call" | custom-call | tf_op jit(solution)/shard_map/pallas_call | solution.py:170
  25.9 1.3 %reshape.10 = f32[2,1024]{1,0:T(2,128)} reshape(f32[16,128]{1,0:T(8,128)} %get-tuple-element.4) | data formatting | bytes 16384 | tf_op jit(solution)/shard_map/reshape | solution.py:199
  27.2 1.3 %copy.7 = f32[1024]{0:T(1024)} copy(f32[1024]{0:T(1024)} %bitcast.1) | data formatting | bytes 8192

commit v2 on v1

--- a/solution.py
+++ b/solution.py
@@ -9,19 +9,22 @@
 
 ITERS = 3
 MESH = pl.DeviceIdType.MESH
-TRANSPOSED = (((1,), (1,)), ((), ()))
 
 
 def kernel(
     regions,
     groups,
-    dirty_ref,
+    dirty_hbm,
     psf_hbm,
-    col_ref,
-    live_ref,
+    col_hbm,
+    live_hbm,
     est_ref,
     broad_ref,
     psf,
+    turned,
+    dirty_ref,
+    col_ref,
+    live_ref,
     target_ref,
     outgoing,
     arrived,
@@ -39,14 +42,6 @@
     freq_count, row_blocks, slots, width = psf.shape[:4]
     rows = freq_count * row_blocks
 
-    first = pltpu.make_async_copy(
-        psf_hbm.at[:, :, pl.ds(0, 1)], psf.at[:, :, pl.ds(0, 1)], load_sem.at[0]
-    )
-    rest = pltpu.make_async_copy(
-        psf_hbm.at[:, :, pl.ds(1, slots - 1)], psf.at[:, :, pl.ds(1, slots - 1)], load_sem.at[1]
-    )
-    first.start()
-    rest.start()
     barrier = pltpu.get_barrier_semaphore()
     for step in range(1, regions):
         pl.semaphore_signal(
@@ -57,6 +52,25 @@
             barrier, inc=1, device_id={"freq": lax.rem(group + step, groups)}, device_id_type=MESH
         )
 
+    first = pltpu.make_async_copy(
+        psf_hbm.at[:, :, pl.ds(0, 1)], psf.at[:, :, pl.ds(0, 1)], load_sem.at[0]
+    )
+    rest = pltpu.make_async_copy(
+        psf_hbm.at[:, :, pl.ds(1, slots - 1)], psf.at[:, :, pl.ds(1, slots - 1)], load_sem.at[1]
+    )
+    first.start()
+    small = [
+        pltpu.make_async_copy(source, target, load_sem.at[2 + n])
+        for n, (source, target) in enumerate(
+            ((dirty_hbm, dirty_ref), (live_hbm, live_ref), (col_hbm, col_ref))
+        )
+    ]
+    for copy in small:
+        copy.start()
+    rest.start()
+
+    for copy in small:
+        copy.wait()
     for f in range(freq_count):
         for i in range(row_blocks):
             row = f * row_blocks + i
@@ -98,15 +112,17 @@
                 device_id={"region": lax.rem(me + step, regions)},
                 device_id_type=MESH,
             ).start()
+        if iteration == 0:
+            rest.wait()
+            for f in range(freq_count):
+                for i in range(row_blocks):
+                    for k in range(1, slots):
+                        turned[f, i, (k - 1) * width : k * width, :] = psf[f, i, k].T
         applied = jnp.zeros((rows, width), jnp.float32)
         for f in range(freq_count):
             for i in range(row_blocks):
-                product = lax.dot_general(
-                    coarse, psf[f, i, 0], TRANSPOSED, preferred_element_type=jnp.float32
-                )
+                product = jnp.dot(coarse, psf[f, i, 0], preferred_element_type=jnp.float32)
                 applied = jnp.where(row_ids == f * row_blocks + i, product, applied)
-        if iteration == 0:
-            rest.wait()
         others = arrived.at[iteration, pl.ds(0, regions - 1)]
         pltpu.make_async_copy(others, others, recv_sem.at[iteration]).wait()
         arrived[iteration, me] = coarse
@@ -125,10 +141,7 @@
         far = jnp.zeros((rows, width), jnp.float32)
         for f in range(freq_count):
             for i in range(row_blocks):
-                blocks = jnp.concatenate([psf[f, i, k] for k in range(1, slots)], axis=1)
-                product = lax.dot_general(
-                    chosen, blocks, TRANSPOSED, preferred_element_type=jnp.float32
-                )
+                product = jnp.dot(chosen, turned[f, i], preferred_element_type=jnp.float32)
                 far = jnp.where(row_ids == f * row_blocks + i, product, far)
         estimate = jnp.maximum(0.0, estimate + (target - (applied + far)) / diagonal)
 
@@ -148,7 +161,10 @@
         )
         copy.start()
         broad.append(copy)
-    est_ref[...] = estimate
+    for f in range(freq_count):
+        for i in range(row_blocks):
+            row = f * row_blocks + i
+            est_ref[f : f + 1, i * width : (i + 1) * width] = estimate[row : row + 1]
     for iteration in range(ITERS):
         others = arrived.at[iteration, pl.ds(0, regions - 1)]
         pltpu.make_async_copy(others, others, send_sem.at[iteration]).wait()
@@ -160,6 +176,17 @@
     broad_ref[...] = total
 
 
+def write_out(est_ref, broad_ref, est_out, broad_out, sems):
+    copies = [
+        pltpu.make_async_copy(est_ref, est_out, sems.at[0]),
+        pltpu.make_async_copy(broad_ref, broad_out, sems.at[1]),
+    ]
+    for copy in copies:
+        copy.start()
+    for copy in copies:
+        copy.wait()
+
+
 def solution(mesh):
     regions, groups = mesh.shape["region"], mesh.shape["freq"]
 
@@ -167,28 +194,25 @@
         freq_count, row_blocks, slots, width, _ = psf_blocks.shape
         rows = freq_count * row_blocks
         vmem = pl.BlockSpec(memory_space=pltpu.VMEM)
+        anywhere = pl.BlockSpec(memory_space=pl.ANY)
         estimate, broadband = pl.pallas_call(
             functools.partial(kernel, regions, groups),
-            out_shape=(
-                jax.ShapeDtypeStruct((rows, width), jnp.float32),
-                jax.ShapeDtypeStruct((row_blocks, width), jnp.float32),
-            ),
-            in_specs=[
-                vmem,
-                pl.BlockSpec(memory_space=pl.ANY),
-                pl.BlockSpec(memory_space=pltpu.SMEM),
-                vmem,
-            ],
+            out_shape=(pltpu.VMEM(dirty_map.shape, jnp.float32), pltpu.VMEM((row_blocks, width), jnp.float32)),
+            in_specs=[anywhere] * 4,
             out_specs=(vmem, vmem),
             scratch_shapes=[
                 pltpu.VMEM(psf_blocks.shape, jnp.bfloat16),
+                pltpu.VMEM((freq_count, row_blocks, (slots - 1) * width, width), jnp.bfloat16),
+                pltpu.VMEM(dirty_map.shape, jnp.float32),
+                pltpu.SMEM(col_index.shape, jnp.int32),
+                pltpu.VMEM(block_live.shape, jnp.int32),
                 pltpu.VMEM((rows, width), jnp.float32),
                 pltpu.VMEM((ITERS, rows, width), jnp.bfloat16),
                 pltpu.VMEM((ITERS, regions, rows, width), jnp.bfloat16),
                 pltpu.VMEM((regions, rows, width), jnp.float32),
                 pltpu.VMEM((rows, (slots - 1) * width), jnp.float32),
                 pltpu.VMEM((groups, row_blocks, width), jnp.float32),
-                pltpu.SemaphoreType.DMA((2,)),
+                pltpu.SemaphoreType.DMA((5,)),
                 pltpu.SemaphoreType.DMA((ITERS,)),
                 pltpu.SemaphoreType.DMA((ITERS,)),
                 pltpu.SemaphoreType.DMA((groups,)),
@@ -196,7 +220,20 @@
             ],
             compiler_params=pltpu.CompilerParams(collective_id=0, has_side_effects=True),
         )(dirty_map, psf_blocks, col_index, block_live)
-        return estimate.reshape(freq_count, row_blocks * width), broadband.reshape(-1)
+        estimate, broadband = pl.pallas_call(
+            write_out,
+            out_shape=(
+                jax.ShapeDtypeStruct(dirty_map.shape, jnp.float32),
+                jax.ShapeDtypeStruct((row_blocks, width), jnp.float32),
+            ),
+            in_specs=[vmem, vmem],
+            out_specs=(anywhere, anywhere),
+            scratch_shapes=[pltpu.SemaphoreType.DMA((2,))],
+        )(
+            pltpu.with_memory_space_constraint(estimate, pltpu.VMEM),
+            pltpu.with_memory_space_constraint(broadband, pltpu.VMEM),
+        )
+        return estimate, broadband.reshape(-1)
 
     return jax.shard_map(
         local,

time: 28.7 us -> 24.3 us (0.85)
  local copies, waits for them, and re-layouts: 2.57 us -> 0 us
  Pallas kernels: 25.2 us -> 23.5 us
    pallas_call x1 -> x2, Pallas kernels: 25.2 us -> 23.5 us  [the longest x1 22.9 us: local(): pl.pallas_call(functools.partial(kernel, regions, groups), out_shape=(plt...]
    reshape x1 -> x0, local copies, waits for them, and re-layouts: 1.3 us -> none  [local(): estimate.reshape(freq_count, row_blocks * width)]
    unnamed x1 -> x0, local copies, waits for them, and re-layouts: 1.26 us -> none
where the time goes in v2:
time: 24.3 us; the launch traced here: 24.2 us
  Pallas kernels  23.5 us (97%)
  between operations  0.64 us (3%)
    pallas_call x1, Pallas kernels, local(): pl.pallas_call(functools.partial(kernel, regions, groups), out_shape=(plt...  22.9 us
    pallas_call x1, Pallas kernels, local(): pl.pallas_call(write_out, out_shape=(jax.ShapeDtypeStruct(dirty_map.shape...  0.62 us

profile of v2, /device:TPU:0, one launch (start us, length us, event | category | flops | bytes accessed | tf_op | source)
XLA Modules:
  0.0 24.2 jit_solution(16226034227116883221)
XLA Ops:
  0.6 22.9 %shard_map.59 = (f32[2,1024]{1,0:T(2,128)S(1)}, f32[8,128]{1,0:T(8,128)S(1)}) custom-call(f32[2,1024]{1,0:T(2,128)} %dirty_hbm.1, bf16[2,8,7,128,128]{4,3,2,1,0:T(8,128)(2,1)} %psf_hbm.1, s32[8,7]{1,0:T(8,128)} %col_hbm.1, s32[8,7]{1,0:T(8,128)} %live_hbm.1), custom_call_target="tpu_custom_call" | custom-call | tf_op jit(solution)/shard_map/pallas_call | solution.py:198
  23.5 0.6 %shard_map.60 = (f32[2,1024]{1,0:T(2,128)}, f32[8,128]{1,0:T(8,128)}) custom-call(f32[2,1024]{1,0:T(2,128)S(1)} %get-tuple-element.6.est_ref, f32[8,128]{1,0:T(8,128)S(1)} %get-tuple-element.7.broad_ref), custom_call_target="tpu_custom_call" | custom-call | tf_op jit(solution)/shard_map/pallas_call | solution.py:223

commit v3 on v2

--- a/solution.py
+++ b/solution.py
@@ -9,6 +9,19 @@
 
 ITERS = 3
 MESH = pl.DeviceIdType.MESH
+
+
+def partners(me, regions):
+    if regions & (regions - 1):
+        return [lax.rem(me + step, regions) for step in range(1, regions)]
+    moves, bit = [], 1
+    while bit < regions:
+        moves.append(bit - 2 * bit * ((me // bit) % 2))
+        bit *= 2
+    return [
+        sum((move for n, move in enumerate(moves) if mask >> n & 1), me)
+        for mask in range(regions - 1, 0, -1)
+    ]
 
 
 def kernel(
@@ -39,26 +52,27 @@
 ):
     me = lax.axis_index("region")
     group = lax.axis_index("freq")
+    peers = partners(me, regions)
     freq_count, row_blocks, slots, width = psf.shape[:4]
     rows = freq_count * row_blocks
 
+    first = pltpu.make_async_copy(
+        psf_hbm.at[:, :, pl.ds(0, 1)], psf.at[:, :, pl.ds(0, 1)], load_sem.at[0]
+    )
+    first.start()
     barrier = pltpu.get_barrier_semaphore()
-    for step in range(1, regions):
+    for peer in peers:
         pl.semaphore_signal(
-            barrier, inc=1, device_id={"region": lax.rem(me + step, regions)}, device_id_type=MESH
+            barrier, inc=1, device_id={"region": peer}, device_id_type=MESH
         )
     for step in range(1, groups):
         pl.semaphore_signal(
             barrier, inc=1, device_id={"freq": lax.rem(group + step, groups)}, device_id_type=MESH
         )
 
-    first = pltpu.make_async_copy(
-        psf_hbm.at[:, :, pl.ds(0, 1)], psf.at[:, :, pl.ds(0, 1)], load_sem.at[0]
-    )
     rest = pltpu.make_async_copy(
         psf_hbm.at[:, :, pl.ds(1, slots - 1)], psf.at[:, :, pl.ds(1, slots - 1)], load_sem.at[1]
     )
-    first.start()
     small = [
         pltpu.make_async_copy(source, target, load_sem.at[2 + n])
         for n, (source, target) in enumerate(
@@ -98,26 +112,30 @@
             diagonal = jnp.where(row_ids == f * row_blocks + i, line, diagonal)
     estimate = jnp.maximum(0.0, target / diagonal)
 
-    for iteration in range(ITERS):
-        coarse = estimate.astype(jnp.bfloat16)
-        outgoing[iteration] = coarse
-        if iteration == 0:
-            pl.semaphore_wait(barrier, regions - 1 + groups - 1)
-        for step in range(1, regions):
+    def send(iteration):
+        for peer in peers:
             pltpu.make_async_remote_copy(
                 src_ref=outgoing.at[iteration],
                 dst_ref=arrived.at[iteration, me],
                 send_sem=send_sem.at[iteration],
                 recv_sem=recv_sem.at[iteration],
-                device_id={"region": lax.rem(me + step, regions)},
+                device_id={"region": peer},
                 device_id_type=MESH,
             ).start()
-        if iteration == 0:
-            rest.wait()
-            for f in range(freq_count):
-                for i in range(row_blocks):
-                    for k in range(1, slots):
-                        turned[f, i, (k - 1) * width : k * width, :] = psf[f, i, k].T
+
+    outgoing[0] = estimate.astype(jnp.bfloat16)
+    pl.semaphore_wait(barrier, regions - 1 + groups - 1)
+    send(0)
+    rest.wait()
+    def turn(row, carry):
+        f, i = row // row_blocks, row % row_blocks
+        for k in range(1, slots):
+            turned[f, i, (k - 1) * width : k * width, :] = psf[f, i, k].T
+        return carry
+
+    lax.fori_loop(0, rows, turn, 0)
+    def sweep(iteration, estimate):
+        coarse = estimate.astype(jnp.bfloat16)
         applied = jnp.zeros((rows, width), jnp.float32)
         for f in range(freq_count):
             for i in range(row_blocks):
@@ -140,11 +158,22 @@
         chosen = (picked[...] * alive).astype(jnp.bfloat16)
         far = jnp.zeros((rows, width), jnp.float32)
         for f in range(freq_count):
-            for i in range(row_blocks):
-                product = jnp.dot(chosen, turned[f, i], preferred_element_type=jnp.float32)
-                far = jnp.where(row_ids == f * row_blocks + i, product, far)
+            for i in range(0, row_blocks, 2):
+                blocks = jnp.concatenate([turned[f, i], turned[f, i + 1]], axis=1)
+                product = jnp.dot(chosen, blocks, preferred_element_type=jnp.float32)
+                for j in range(2):
+                    part = product[:, j * width : (j + 1) * width]
+                    far = jnp.where(row_ids == f * row_blocks + i + j, part, far)
         estimate = jnp.maximum(0.0, estimate + (target - (applied + far)) / diagonal)
 
+        @pl.when(iteration < ITERS - 1)
+        def _():
+            outgoing[iteration + 1] = estimate.astype(jnp.bfloat16)
+            send(iteration + 1)
+
+        return estimate
+
+    estimate = lax.fori_loop(0, ITERS, sweep, estimate)
     local_sum = estimate[:row_blocks]
     for f in range(1, freq_count):
         local_sum = local_sum + estimate[f * row_blocks : (f + 1) * row_blocks]

time: 24.3 us -> 23.9 us (0.984)
  Pallas kernels: 23.5 us -> 23.1 us
    pallas_call x1, Pallas kernels: 22.9 us -> 22.5 us  [local(): pl.pallas_call(functools.partial(kernel, regions, groups), out_shape=(plt...]
where the time goes in v3:
time: 23.9 us; the launch traced here: 23.7 us
  Pallas kernels  23.1 us (97%)
  between operations  0.64 us (3%)
    pallas_call x1, Pallas kernels, local(): pl.pallas_call(functools.partial(kernel, regions, groups), out_shape=(plt...  22.5 us
    pallas_call x1, Pallas kernels, local(): pl.pallas_call(write_out, out_shape=(jax.ShapeDtypeStruct(dirty_map.shape...  0.62 us

profile of v3, /device:TPU:0, one launch (start us, length us, event | category | flops | bytes accessed | tf_op | source)
XLA Modules:
  0.0 23.7 jit_solution(14629737116916243417)
XLA Ops:
  0.6 22.5 %shard_map.59 = (f32[2,1024]{1,0:T(2,128)S(1)}, f32[8,128]{1,0:T(8,128)S(1)}) custom-call(f32[2,1024]{1,0:T(2,128)} %dirty_hbm.1, bf16[2,8,7,128,128]{4,3,2,1,0:T(8,128)(2,1)} %psf_hbm.1, s32[8,7]{1,0:T(8,128)} %col_hbm.1, s32[8,7]{1,0:T(8,128)} %live_hbm.1), custom_call_target="tpu_custom_call" | custom-call | tf_op jit(solution)/shard_map/pallas_call | solution.py:227
  23.1 0.6 %shard_map.60 = (f32[2,1024]{1,0:T(2,128)}, f32[8,128]{1,0:T(8,128)}) custom-call(f32[2,1024]{1,0:T(2,128)S(1)} %get-tuple-element.6.est_ref, f32[8,128]{1,0:T(8,128)S(1)} %get-tuple-element.7.broad_ref), custom_call_target="tpu_custom_call" | custom-call | tf_op jit(solution)/shard_map/pallas_call | solution.py:252
